TPU v7x, 512 devices: a whole 4x8x8 slice. The times are simulated.
512 devices in a mesh: leaf: 32 (over y, x), col: 16 (over z, core).
Axes of the slice: x: 4, y: 8, z: 8, core: 2. Of those that a mesh axis runs over, the one named last changes fastest.
Arguments:
- points: float32 [3, 262144], P(None, ('leaf', 'col'))
- point_ids: int32 [262144], P(('leaf', 'col')), may hold values from 0 to 1048575, as said below
- signs: int32 [262144], P(('leaf', 'col')), may hold values from 0 to 1
- hadamard_sample_rows: int32 [512], replicated, may hold values from 0 to 1048575, as said below
- samples: bfloat16 [262144, 512], P(('leaf', 'col')), may hold values from -6 to 6
- skeleton: int32 [60, 128], replicated, may hold values from 0 to 8191, as said below
- ranks: int32 [60], replicated, may hold values from 64 to 128, as said below
Outputs:
- leaf_basis: bfloat16 [262144, 128], P(('leaf', 'col'))
- top_sample: float32 [512, 512], P('leaf', 'col')
- top_omega: float32 [512, 512], P('leaf', 'col')
Inputs may be any that keep to these rules, and one draw needn't show every extreme that they name: `point_ids`: increasing and distinct; the first is 0 and the last 1048575. `hadamard_sample_rows`: increasing and distinct; the first is 0 and the last 1048575. `skeleton`: each row holds distinct indices; in the first 32 rows (leaves) they are below 8192, in the others below 256; entry i of a leaf row lies in [i * 64, (i + 1) * 64). `ranks`: some node has rank 128 and some other node rank 128 / 2.
All inputs are finite; a program needn't handle non-finite values.
Results may differ from a plain program's by a relative error of at most 0.0018.
Values sent between devices are 32-bit elements; how exact they have to be, the bound alone decides.
A program may use at most 64 MiB of HBM per device.

v0:
```python
import jax
import jax.numpy as jnp
from jax import lax
from jax.sharding import PartitionSpec as P

NTOTAL = 1048576
KERNEL_SCALE = 1.0
OMEGA_UNIT = 0.0625
RIDGE = 0.25
HIGH = lax.Precision.HIGHEST


def swapped(value, axis, bit):
    mask = 2**bit
    pairs = [(source, source ^ mask) for source in range(lax.axis_size(axis))]
    return lax.ppermute(value, axis, pairs)


def omega_rows(tags, hadamard_sample_rows, bit_count):
    powers = jnp.array([1 << shift for shift in range(bit_count)], dtype=jnp.int32)
    row_bits = (tags[0][:, None] // powers[None, :] % 2).astype(jnp.float32)
    col_bits = (hadamard_sample_rows[None, :] // powers[:, None] % 2).astype(jnp.float32)
    counted = jnp.dot(row_bits, col_bits, precision=HIGH)
    parity = counted - 2.0 * jnp.floor(0.5 * counted)
    flips = (2 * tags[1] - 1).astype(jnp.float32)
    return (1.0 - 2.0 * parity) * flips[:, None] * OMEGA_UNIT


def kernel_tile(left, right):
    squared_distance = jnp.zeros((left.shape[1], right.shape[1]), jnp.float32)
    for axis_k in range(3):
        offset = left[axis_k][:, None] - right[axis_k][None, :]
        squared_distance = squared_distance + offset * offset
    return jnp.exp(-KERNEL_SCALE * squared_distance)


def ridge_fit(picked, gram, rank):
    shift = RIDGE * jnp.trace(gram) / rank.astype(jnp.float32) + 1e-06
    ident = jnp.eye(gram.shape[0], dtype=jnp.float32)
    factor = jnp.linalg.cholesky(gram + shift * ident)
    return jax.scipy.linalg.cho_solve((factor, True), picked)


def local(points, point_ids, signs, hadamard_sample_rows, samples, skeleton, ranks):
    leaf_count = lax.axis_size("leaf")
    col_count = lax.axis_size("col")
    leaf_pos = lax.axis_index("leaf")
    col_pos = lax.axis_index("col")
    rows = points.shape[1]
    width = samples.shape[1]
    rank_limit = skeleton.shape[1]
    bit_count = NTOTAL.bit_length() - 1
    tags = jnp.stack([point_ids, signs])
    own_omega = omega_rows(tags, hadamard_sample_rows, bit_count)
    distant_points = lax.all_gather(points, "col", axis=1, tiled=True)
    far_tags = lax.all_gather(tags, "col", axis=1, tiled=True)
    block_omega = omega_rows(far_tags, hadamard_sample_rows, bit_count).astype(jnp.bfloat16)
    tile = kernel_tile(points, distant_points).astype(jnp.bfloat16)
    near = jnp.dot(tile, block_omega, preferred_element_type=jnp.float32)
    residue = samples.astype(jnp.float32) - near
    positions = jnp.arange(rank_limit, dtype=jnp.int32)
    leaf_skel = skeleton[leaf_pos] - col_pos * rows
    leaf_rank = ranks[leaf_pos]
    keep = (positions < leaf_rank).astype(jnp.float32)
    chooser = (leaf_skel[:, None] == jnp.arange(rows, dtype=jnp.int32)[None, :]).astype(jnp.float32)
    part_picked = jnp.dot(chooser, residue, precision=HIGH) * keep[:, None]
    part_spots = jnp.dot(points, chooser.T, precision=HIGH)
    picked, spots = lax.psum((part_picked, part_spots), "col")
    gram = jnp.dot(picked, picked.T, precision=HIGH)
    fitted = ridge_fit(picked, gram, leaf_rank)
    basis = jnp.dot(residue, fitted.T, precision=HIGH)
    projected = lax.psum(jnp.dot(basis.T, own_omega, precision=HIGH), "col")
    leaf_basis = basis.astype(jnp.bfloat16)
    span = width // col_count
    base = 0
    for level in range(1, 4):
        child_base = base
        base = base + (leaf_count >> level - 1)
        sibling_selected, other_proj, other_spots = swapped(
            (picked, projected, spots), "leaf", level - 1
        )
        is_left = leaf_pos // (1 << level - 1) % 2 == 0
        left_picked = jnp.where(is_left, picked, sibling_selected)
        right_picked = jnp.where(is_left, sibling_selected, picked)
        left_proj = jnp.where(is_left, projected, other_proj)
        right_proj = jnp.where(is_left, other_proj, projected)
        left_positions = jnp.where(is_left, spots, other_spots)
        right_spots = jnp.where(is_left, other_spots, spots)
        pair_index = leaf_pos // (1 << level)
        left_keep = (positions < ranks[child_base + 2 * pair_index]).astype(jnp.float32)
        right_keep = (positions < ranks[child_base + 2 * pair_index + 1]).astype(jnp.float32)
        cross = kernel_tile(left_positions, right_spots)
        upper = (left_picked - jnp.dot(cross, right_proj, precision=HIGH)) * left_keep[:, None]
        lower = (right_picked - jnp.dot(cross.T, left_proj, precision=HIGH)) * right_keep[:, None]
        candidates = jnp.concatenate([upper, lower], 0)
        stacked = jnp.concatenate([left_proj, right_proj], 0)
        cand_spots = jnp.concatenate([left_positions, right_spots], 1)
        node_skel = skeleton[base + pair_index]
        node_rank = ranks[base + pair_index]
        node_keep = (positions < node_rank).astype(jnp.float32)
        selector = (
            node_skel[:, None] == jnp.arange(2 * rank_limit, dtype=jnp.int32)[None, :]
        ).astype(jnp.float32)
        new_picked = jnp.dot(selector, candidates, precision=HIGH) * node_keep[:, None]
        new_spots = jnp.dot(cand_spots, selector.T, precision=HIGH)
        gram = jnp.dot(new_picked, new_picked.T, precision=HIGH)
        fitted = ridge_fit(new_picked, gram, node_rank)
        parent_basis = jnp.dot(candidates, fitted.T, precision=HIGH)
        projected = jnp.dot(parent_basis.T, stacked, precision=HIGH)
        picked = new_picked
        spots = new_spots
    picked = lax.dynamic_slice_in_dim(picked, col_pos * span, span, 1)
    projected = lax.dynamic_slice_in_dim(projected, col_pos * span, span, 1)
    share = rank_limit // 8
    top_sample = lax.dynamic_slice_in_dim(picked, leaf_pos % 8 * share, share, 0)
    top_omega = lax.dynamic_slice_in_dim(projected, leaf_pos % 8 * share, share, 0)
    return (leaf_basis, top_sample, top_omega)


def solution(mesh):
    placed = (
        P(None, ("leaf", "col")),
        P(("leaf", "col")),
        P(("leaf", "col")),
        P(),
        P(("leaf", "col"), None),
        P(),
        P(),
    )
    return jax.shard_map(
        local,
        mesh=mesh,
        in_specs=placed,
        out_specs=(P(("leaf", "col"), None), P("leaf", "col"), P("leaf", "col")),
        check_vma=False,
    )
```

profile of v0, /device:TPU:2, one launch (start us, length us, event | category | flops | bytes accessed | tf_op | source)
XLA Modules:
  0.0 488.6 jit_solution(7445075124836231805)
XLA Ops:
  7.2 23.8 %all_gather.6 = f32[3,8192]{1,0:T(4,128)S(1)} all-gather(f32[3,512]{1,0:T(4,128)} %param.14), channel_id=1, replica_groups=mesh['leaf'=32,'col'=16] {'col'}, dimensions={1}, use_global_device_ids=true | all-gather | bytes 104448 | tf_op jit(solution)/shard_map/all_gather | solution.py:55
  32.5 14.6 %all_gather.7 = s32[2,8192]{1,0:T(2,128)S(1)} all-gather(s32[2,512]{1,0:T(2,128)S(1)} %pad_add_fusion), channel_id=1, replica_groups=mesh['leaf'=32,'col'=16] {'col'}, dimensions={1}, use_global_device_ids=true | all-gather | bytes 69632 | tf_op jit(solution)/shard_map/all_gather | solution.py:56
  51.2 29.2 %multiply_convert_fusion = bf16[8192,512]{1,0:T(8,128)(2,1)S(1)} fusion(f32[8192]{0:T(1024)S(1)} %bitcast.150, s32[20]{0:T(128)} %constant.260.clone, s32[8192]{0:T(1024)S(1)} %bitcast.146, pred[8192]{0:T(1024)(128)(4,1)S(1)} %sign_compare_fusion, s32[512]{0:T(512)} %param.17, pred[512]{0:T(512)(128)(4,1)S(1)} %compare_reduce_fusion), kind=kOutput, calls=%fused_computation | convolution fusion | flops 1047515136 | bytes 8464976 | tf_op jit(solution)/shard_map/dot_general | solution.py:23
  80.5 6.7 %fusion.8 = f32[512,512]{1,0:T(8,128)S(1)} fusion(bf16[8192,512]{1,0:T(8,128)(2,1)S(1)} %multiply_convert_fusion, f32[8192]{0:T(1024)S(1)} %bitcast.148, f32[512]{0:T(512)S(1)} %bitcast.156, f32[8192]{0:T(1024)S(1)} %bitcast.149, f32[512]{0:T(512)S(1)} %bitcast.155, f32[8192]{0:T(1024)S(1)} %bitcast.147, f32[512]{0:T(512)S(1)} %bitcast.154, ...), kind=kOutput, calls=%fused_computation.10 | convolution fusion | flops 4337434624 | bytes 10065920 | tf_op jit(solution)/shard_map/dot_general | solution.py:59
  88.8 25.2 %psum.22 = f32[3,128]{1,0:T(4,128)S(1)} all-reduce(f32[3,128]{1,0:T(4,128)S(1)} %convolution_bitcast_fusion), channel_id=1, replica_groups=mesh['leaf'=32,'col'=16] {'col'}, use_global_device_ids=true, to_apply=%region_4.8 | all-reduce | flops 384 | bytes 3072 | tf_op jit(solution)/shard_map/psum | solution.py:68
  119.5 4.1 fusion.54
  129.5 72.7 %all-reduce.3.cloned.1.call-done = f32[128,512]{1,0:T(8,128)} async-done(((f32[128,512]{1,0:T(8,128)}), f32[128,512]{1,0:T(8,128)}) %all-reduce.3.cloned.1.call-update) | async-done | bytes 262160 | tf_op jit(solution)/shard_map/psum | solution.py:68
  205.0 11.7 %cholesky.74 = f32[128,128]{1,0:T(8,128)S(1)} custom-call(f32[128,128]{1,0:T(8,128)S(1)} %fusion.94), custom_call_target="Cholesky" | custom-call | tf_op jit(solution)/shard_map/jit(cholesky)/cholesky | solution.py:40
  218.1 9.8 %custom-call.10 = f32[1,128,128]{1,2,0:T(8,128)S(1)} custom-call(f32[1,128,128]{2,1,0:T(8,128)S(1)} %fusion.71), custom_call_target="InvertDiagBlocksLowerTriangular" | custom-call | tf_op jit(solution)/shard_map/jit(_cho_solve)/triangular_solve | solution.py:41
  233.5 4.0 collective-permute-start.4
  237.5 111.8 %all-reduce.5.cloned.1.call-done = f32[128,512]{1,0:T(8,128)} async-done(((f32[128,512]{1,0:T(8,128)}), f32[128,512]{1,0:T(8,128)}) %all-reduce.5.cloned.1.call-update) | async-done | bytes 262160 | tf_op jit(solution)/shard_map/psum | solution.py:72
  355.2 5.4 %collective-permute-done.2 = f32[128,512]{1,0:T(8,128)S(1)} collective-permute-done((f32[128,512]{1,0:T(8,128)}, f32[128,512]{1,0:T(8,128)S(1)}, u32[]{:S(2)}, u32[]{:S(2)}) %collective-permute-start.2) | collective-permute-done | bytes 262176 | tf_op jit(solution)/shard_map/ppermute | solution.py:16
  361.6 3.5 collective-permute-done
  369.3 11.7 %cholesky.85 = f32[128,128]{1,0:T(8,128)S(1)} custom-call(f32[128,128]{1,0:T(8,128)S(1)} %fusion.89), custom_call_target="Cholesky" | custom-call | tf_op jit(solution)/shard_map/jit(cholesky)/cholesky | solution.py:40
  382.3 9.8 %custom-call.11 = f32[1,128,128]{1,2,0:T(8,128)S(1)} custom-call(f32[1,128,128]{2,1,0:T(8,128)S(1)} %fusion.72), custom_call_target="InvertDiagBlocksLowerTriangular" | custom-call | tf_op jit(solution)/shard_map/jit(_cho_solve)/triangular_solve | solution.py:41
  394.0 4.0 collective-permute-start.5
  401.6 3.7 collective-permute-start.7
  406.6 3.7 collective-permute-done.3
  413.4 11.7 %cholesky.96 = f32[128,128]{1,0:T(8,128)S(1)} custom-call(f32[128,128]{1,0:T(8,128)S(1)} %fusion.84), custom_call_target="Cholesky" | custom-call | tf_op jit(solution)/shard_map/jit(cholesky)/cholesky | solution.py:40
  426.5 9.8 %custom-call.12 = f32[1,128,128]{1,2,0:T(8,128)S(1)} custom-call(f32[1,128,128]{2,1,0:T(8,128)S(1)} %fusion.73), custom_call_target="InvertDiagBlocksLowerTriangular" | custom-call | tf_op jit(solution)/shard_map/jit(_cho_solve)/triangular_solve | solution.py:41
  438.2 3.4 collective-permute-start.8
  444.3 4.7 collective-permute-done.8
  455.3 11.7 %cholesky.107 = f32[128,128]{1,0:T(8,128)S(1)} custom-call(f32[128,128]{1,0:T(8,128)S(1)} %fusion.79), custom_call_target="Cholesky" | custom-call | tf_op jit(solution)/shard_map/jit(cholesky)/cholesky | solution.py:40
  468.3 9.8 %custom-call.13 = f32[1,128,128]{1,2,0:T(8,128)S(1)} custom-call(f32[1,128,128]{2,1,0:T(8,128)S(1)} %fusion.74), custom_call_target="InvertDiagBlocksLowerTriangular" | custom-call | tf_op jit(solution)/shard_map/jit(_cho_solve)/triangular_solve | solution.py:41
  (116 shorter events, 61.4 us)
Async XLA Ops:
  7.2 194.9 %all-reduce.3.cloned.1.call-start = ((), (), s32[]{:S(2)}) async-start(), calls=%async_computation | async-start | bytes 524288 | tf_op jit(solution)/shard_map/psum | solution.py:68
  51.2 29.2 %copy-start.5 = (bf16[512,512]{1,0:T(8,128)(2,1)S(1)}, bf16[512,512]{1,0:T(8,128)(2,1)}, u32[]{:S(2)}) copy-start(bf16[512,512]{1,0:T(8,128)(2,1)} %param.18) | copy-start | bytes 1572868
  80.4 8.1 %copy-start.1 = (f32[3,512]{1,0:T(4,128)S(1)}, f32[3,512]{1,0:T(4,128)}, u32[]{:S(2)}) copy-start(f32[3,512]{1,0:T(4,128)} %param.14) | copy-start | bytes 18436
  80.4 37.1 %copy-start.2 = (s32[512]{0:T(512)S(1)}, s32[512]{0:T(512)}, u32[]{:S(2)}) copy-start(s32[512]{0:T(512)} %param.15) | copy-start | bytes 6148
  80.4 37.1 %copy-start.3 = (s32[512]{0:T(512)S(1)}, s32[512]{0:T(512)}, u32[]{:S(2)}) copy-start(s32[512]{0:T(512)} %param.16) | copy-start | bytes 6148
  80.5 39.0 %copy-start.4 = (s32[512]{0:T(512)S(1)}, s32[512]{0:T(512)}, u32[]{:S(2)}) copy-start(s32[512]{0:T(512)} %param.17) | copy-start | bytes 6148
  80.5 39.0 %copy-start.6 = (s32[20]{0:T(128)S(1)}, s32[20]{0:T(128)}, u32[]{:S(2)}) copy-start(s32[20]{0:T(128)} %constant.260.clone) | copy-start | bytes 244
  88.5 260.9 %all-reduce.5.cloned.1.call-start = ((), (), s32[]{:S(2)}) async-start(), calls=%async_computation.1 | async-start | bytes 524288 | tf_op jit(solution)/shard_map/psum | solution.py:72
  114.0 15.5 %collective-permute-start.1 = (f32[3,128]{1,0:T(4,128)S(1)}, f32[3,128]{1,0:T(4,128)S(1)}, u32[]{:S(2)}, u32[]{:S(2)}) collective-permute-start(f32[3,128]{1,0:T(4,128)S(1)} %psum.22), channel_id=1, source_target_pairs={{0,16},{16,0},{32,48},{48,32},{64,80},{80,64},{96,112},{112,96},{1... | collective-permute-start | bytes 4616 | tf_op jit(solution)/shard_map/ppermute | solution.py:16
  202.1 164.5 %copy-start = (f32[128,512]{1,0:T(8,128)S(1)}, f32[128,512]{1,0:T(8,128)}, u32[]{:S(2)}) copy-start(f32[128,512]{1,0:T(8,128)} %all-reduce.3.cloned.1.call-done) | copy-start | bytes 786436
  233.5 121.7 %collective-permute-start.4 = (f32[3,128]{1,0:T(4,128)S(1)}, f32[3,128]{1,0:T(4,128)S(1)}, u32[]{:S(2)}, u32[]{:S(2)}) collective-permute-start(f32[3,128]{1,0:T(4,128)S(1)} %fusion.66), channel_id=1, source_target_pairs={{0,32},{16,48},{32,0},{48,16},{64,96},{80,112},{96,64},{112,80},{1... | collective-permute-start | bytes 4616 | tf_op jit(solution)/shard_map/ppermute | solution.py:16
  349.3 11.3 %collective-permute-start.2 = (f32[128,512]{1,0:T(8,128)}, f32[128,512]{1,0:T(8,128)S(1)}, u32[]{:S(2)}, u32[]{:S(2)}) collective-permute-start(f32[128,512]{1,0:T(8,128)} %all-reduce.5.cloned.1.call-done), channel_id=1, source_target_pairs={{0,16},{16,0},{32,48},{48,32},{64,80},{80,64},{96,112},{112,96},{1... | collective-permute-start | bytes 786440 | tf_op jit(solution)/shard_map/ppermute | solution.py:16
  351.8 13.3 %collective-permute-start = (f32[128,512]{1,0:T(8,128)}, f32[128,512]{1,0:T(8,128)S(1)}, u32[]{:S(2)}, u32[]{:S(2)}) collective-permute-start(f32[128,512]{1,0:T(8,128)} %all-reduce.3.cloned.1.call-done), channel_id=1, source_target_pairs={{0,16},{16,0},{32,48},{48,32},{64,80},{80,64},{96,112},{112,96},{1... | collective-permute-start | bytes 786440 | tf_op jit(solution)/shard_map/ppermute | solution.py:16
  394.0 12.5 %collective-permute-start.5 = (f32[128,512]{1,0:T(8,128)S(1)}, f32[128,512]{1,0:T(8,128)S(1)}, u32[]{:S(2)}, u32[]{:S(2)}) collective-permute-start(f32[128,512]{1,0:T(8,128)S(1)} %fusion.25), channel_id=1, source_target_pairs={{0,32},{16,48},{32,0},{48,16},{64,96},{80,112},{96,64},{112,80},{1... | collective-permute-start | bytes 786440 | tf_op jit(solution)/shard_map/ppermute | solution.py:16
  398.0 12.3 %collective-permute-start.3 = (f32[128,512]{1,0:T(8,128)S(1)}, f32[128,512]{1,0:T(8,128)S(1)}, u32[]{:S(2)}, u32[]{:S(2)}) collective-permute-start(f32[128,512]{1,0:T(8,128)S(1)} %convolution_multiply_fusion.2), channel_id=1, source_target_pairs={{0,32},{16,48},{32,0},{48,16},{64,96},{80,112},{96,64},{112,80},{1... | collective-permute-start | bytes 786440 | tf_op jit(solution)/shard_map/ppermute | solution.py:16
  401.6 40.0 %collective-permute-start.7 = (f32[3,128]{1,0:T(4,128)S(1)}, f32[3,128]{1,0:T(4,128)S(1)}, u32[]{:S(2)}, u32[]{:S(2)}) collective-permute-start(f32[3,128]{1,0:T(4,128)S(1)} %fusion.67), channel_id=1, source_target_pairs={{0,64},{16,80},{32,96},{48,112},{64,0},{80,16},{96,32},{112,48},{1... | collective-permute-start | bytes 4616 | tf_op jit(solution)/shard_map/ppermute | solution.py:16
  438.2 10.8 %collective-permute-start.8 = (f32[128,512]{1,0:T(8,128)S(1)}, f32[128,512]{1,0:T(8,128)S(1)}, u32[]{:S(2)}, u32[]{:S(2)}) collective-permute-start(f32[128,512]{1,0:T(8,128)S(1)} %fusion.29), channel_id=1, source_target_pairs={{0,64},{16,80},{32,96},{48,112},{64,0},{80,16},{96,32},{112,48},{1... | collective-permute-start | bytes 786440 | tf_op jit(solution)/shard_map/ppermute | solution.py:16
  441.6 10.5 %collective-permute-start.6 = (f32[128,512]{1,0:T(8,128)S(1)}, f32[128,512]{1,0:T(8,128)S(1)}, u32[]{:S(2)}, u32[]{:S(2)}) collective-permute-start(f32[128,512]{1,0:T(8,128)S(1)} %convolution_multiply_fusion.1), channel_id=1, source_target_pairs={{0,64},{16,80},{32,96},{48,112},{64,0},{80,16},{96,32},{112,48},{1... | collective-permute-start | bytes 786440 | tf_op jit(solution)/shard_map/ppermute | solution.py:16
Sparse Core Ops, SparseCore 0:
  88.6 113.4 all-reduce.2
  233.4 115.8 all-reduce.4
where the time goes:
time: 496 us; the launch traced here: 489 us
  waiting for transfers between devices  206 us (42%)
  other arithmetic  101 us (20%)
  blocking collectives  63.6 us (13%)
  matrix products  62.6 us (13%)
  starting transfers between devices  29.9 us (6%)
  between operations  20.8 us (4%)
    psum x1, waiting for transfers between devices, local(): projected = lax.psum(jnp.dot(basis.T, own_omega, precision=HIGH), 'col')  112 us
    psum x1, waiting for transfers between devices, local(): picked, spots = lax.psum((part_picked, part_spots), 'col')  72.7 us
    another operation x12, other arithmetic, ridge_fit(): factor = jnp.linalg.cholesky(gram + shift * ident)  49.6 us
    another operation x8, other arithmetic, ridge_fit(): return jax.scipy.linalg.cho_solve((factor, True), picked)  41.9 us
    dot_general x2, matrix products, omega_rows(): counted = jnp.dot(row_bits, col_bits, precision=HIGH)  33.3 us
    ppermute x9, starting transfers between devices, swapped(): return lax.ppermute(value, axis, pairs)  29.8 us
    psum x1, blocking collectives, local(): picked, spots = lax.psum((part_picked, part_spots), 'col')  25.2 us
    all_gather x1, blocking collectives, local(): distant_points = lax.all_gather(points, 'col', axis=1, tiled=True)  23.8 us
  transfers between devices with their start and end apart: 11, of which 8 were waited for; matrix products, arithmetic and copies ran while one was open for 8% of the time, Pallas kernels for 0%

commit v1 on v0

--- a/solution.py
+++ b/solution.py
@@ -69,7 +69,9 @@
     gram = jnp.dot(picked, picked.T, precision=HIGH)
     fitted = ridge_fit(picked, gram, leaf_rank)
     basis = jnp.dot(residue, fitted.T, precision=HIGH)
-    projected = lax.psum(jnp.dot(basis.T, own_omega, precision=HIGH), "col")
+    part = jnp.dot(basis.T, own_omega, precision=HIGH)
+    parts = lax.all_gather(part, "col")
+    projected = jnp.sum(parts, axis=0)
     leaf_basis = basis.astype(jnp.bfloat16)
     span = width // col_count
     base = 0

time: 496 us -> 427 us (0.86)
  the two profiles are of different devices: /device:TPU:2 before, /device:TPU:8 now
where the time goes in v1:
time: 427 us; the launch traced here: 420 us
  waiting for transfers between devices  135 us (32%)
  other arithmetic  103 us (24%)
  blocking collectives  65.7 us (15%)
  matrix products  61.6 us (14%)
  starting transfers between devices  30.7 us (7%)
  between operations  20.6 us (5%)
  local copies, waits for them, and re-layouts  4.37 us (1%)
    psum x1, waiting for transfers between devices, local(): picked, spots = lax.psum((part_picked, part_spots), 'col')  108 us
    another operation x12, other arithmetic, ridge_fit(): factor = jnp.linalg.cholesky(gram + shift * ident)  49.6 us
    another operation x8, other arithmetic, ridge_fit(): return jax.scipy.linalg.cho_solve((factor, True), picked)  41.9 us
    dot_general x2, matrix products, omega_rows(): counted = jnp.dot(row_bits, col_bits, precision=HIGH)  33.3 us
    ppermute x9, starting transfers between devices, swapped(): return lax.ppermute(value, axis, pairs)  30 us
    psum x1, blocking collectives, local(): picked, spots = lax.psum((part_picked, part_spots), 'col')  27.4 us
    ppermute x9, waiting for transfers between devices, swapped(): return lax.ppermute(value, axis, pairs)  24.9 us
    all_gather x1, blocking collectives, local(): distant_points = lax.all_gather(points, 'col', axis=1, tiled=True)  23.8 us
  transfers between devices with their start and end apart: 11, of which 8 were waited for; matrix products, arithmetic and copies ran while one was open for 10% of the time, Pallas kernels for 0%

profile of v1, /device:TPU:8, one launch (start us, length us, event | category | flops | bytes accessed | tf_op | source)
XLA Modules:
  0.0 420.4 jit_solution(13305092889439046689)
XLA Ops:
  7.2 23.8 %all_gather.12 = f32[3,8192]{1,0:T(4,128)S(1)} all-gather(f32[3,512]{1,0:T(4,128)} %param.14), channel_id=1, replica_groups=mesh['leaf'=32,'col'=16] {'col'}, dimensions={1}, use_global_device_ids=true | all-gather | bytes 104448 | tf_op jit(solution)/shard_map/all_gather | solution.py:55
  32.5 14.6 %all_gather.13 = s32[2,8192]{1,0:T(2,128)S(1)} all-gather(s32[2,512]{1,0:T(2,128)S(1)} %pad_add_fusion), channel_id=1, replica_groups=mesh['leaf'=32,'col'=16] {'col'}, dimensions={1}, use_global_device_ids=true | all-gather | bytes 69632 | tf_op jit(solution)/shard_map/all_gather | solution.py:56
  51.2 29.2 %multiply_convert_fusion = bf16[8192,512]{1,0:T(8,128)(2,1)S(1)} fusion(f32[8192]{0:T(1024)S(1)} %bitcast.152, s32[20]{0:T(128)} %constant.261.clone, s32[8192]{0:T(1024)S(1)} %bitcast.148, pred[8192]{0:T(1024)(128)(4,1)S(1)} %sign_compare_fusion, s32[512]{0:T(512)} %param.17, pred[512]{0:T(512)(128)(4,1)S(1)} %compare_reduce_fusion), kind=kOutput, calls=%fused_computation | convolution fusion | flops 1047515136 | bytes 8464976 | tf_op jit(solution)/shard_map/dot_general | solution.py:23
  80.4 6.7 %fusion.8 = f32[512,512]{1,0:T(8,128)S(1)} fusion(bf16[8192,512]{1,0:T(8,128)(2,1)S(1)} %multiply_convert_fusion, f32[8192]{0:T(1024)S(1)} %bitcast.150, f32[512]{0:T(512)S(1)} %bitcast.158, f32[8192]{0:T(1024)S(1)} %bitcast.151, f32[512]{0:T(512)S(1)} %bitcast.157, f32[8192]{0:T(1024)S(1)} %bitcast.149, f32[512]{0:T(512)S(1)} %bitcast.156, ...), kind=kOutput, calls=%fused_computation.10 | convolution fusion | flops 4337434624 | bytes 10065920 | tf_op jit(solution)/shard_map/dot_general | solution.py:59
  89.8 4.1 fusion.54
  93.9 108.0 %all-reduce.2.cloned.1.call-done = f32[128,512]{1,0:T(8,128)} async-done(((f32[128,512]{1,0:T(8,128)}), f32[128,512]{1,0:T(8,128)}) %all-reduce.2.cloned.1.call-update) | async-done | bytes 262160 | tf_op jit(solution)/shard_map/psum | solution.py:68
  204.9 11.7 %cholesky.74 = f32[128,128]{1,0:T(8,128)S(1)} custom-call(f32[128,128]{1,0:T(8,128)S(1)} %fusion.94), custom_call_target="Cholesky" | custom-call | tf_op jit(solution)/shard_map/jit(cholesky)/cholesky | solution.py:40
  217.9 9.8 %custom-call.10 = f32[1,128,128]{1,2,0:T(8,128)S(1)} custom-call(f32[1,128,128]{2,1,0:T(8,128)S(1)} %fusion.71), custom_call_target="InvertDiagBlocksLowerTriangular" | custom-call | tf_op jit(solution)/shard_map/jit(_cho_solve)/triangular_solve | solution.py:41
  233.4 27.4 %psum.15 = f32[3,128]{1,0:T(4,128)S(1)} all-reduce(f32[3,128]{1,0:T(4,128)S(1)} %convolution_bitcast_fusion), channel_id=1, replica_groups=mesh['leaf'=32,'col'=16] {'col'}, use_global_device_ids=true, to_apply=%region_4.8 | all-reduce | flops 384 | bytes 3072 | tf_op jit(solution)/shard_map/psum | solution.py:68
  271.9 4.7 %collective-permute-start.4 = (f32[3,128]{1,0:T(4,128)S(1)}, f32[3,128]{1,0:T(4,128)S(1)}, u32[]{:S(2)}, u32[]{:S(2)}) collective-permute-start(f32[3,128]{1,0:T(4,128)S(1)} %fusion.66), channel_id=1, source_target_pairs={{0,32},{16,48},{32,0},{48,16},{64,96},{80,112},{96,64},{112,80},{1... | collective-permute-start | bytes 4616 | tf_op jit(solution)/shard_map/ppermute | solution.py:16
  280.8 3.4 collective-permute-start.2
  286.7 5.2 %collective-permute-done.2 = f32[128,512]{1,0:T(8,128)S(1)} collective-permute-done((f32[128,512]{1,0:T(8,128)S(1)}, f32[128,512]{1,0:T(8,128)S(1)}, u32[]{:S(2)}, u32[]{:S(2)}) %collective-permute-start.2) | collective-permute-done | bytes 262176 | tf_op jit(solution)/shard_map/ppermute | solution.py:16
  291.9 4.8 %collective-permute-done = f32[128,512]{1,0:T(8,128)S(1)} collective-permute-done((f32[128,512]{1,0:T(8,128)S(1)}, f32[128,512]{1,0:T(8,128)S(1)}, u32[]{:S(2)}, u32[]{:S(2)}) %collective-permute-start) | collective-permute-done | bytes 262176 | tf_op jit(solution)/shard_map/ppermute | solution.py:16
  299.9 11.7 %cholesky.85 = f32[128,128]{1,0:T(8,128)S(1)} custom-call(f32[128,128]{1,0:T(8,128)S(1)} %fusion.89), custom_call_target="Cholesky" | custom-call | tf_op jit(solution)/shard_map/jit(cholesky)/cholesky | solution.py:40
  313.0 9.8 %custom-call.11 = f32[1,128,128]{1,2,0:T(8,128)S(1)} custom-call(f32[1,128,128]{2,1,0:T(8,128)S(1)} %fusion.72), custom_call_target="InvertDiagBlocksLowerTriangular" | custom-call | tf_op jit(solution)/shard_map/jit(_cho_solve)/triangular_solve | solution.py:41
  324.6 4.8 %collective-permute-start.5 = (f32[128,512]{1,0:T(8,128)S(1)}, f32[128,512]{1,0:T(8,128)S(1)}, u32[]{:S(2)}, u32[]{:S(2)}) collective-permute-start(f32[128,512]{1,0:T(8,128)S(1)} %fusion.25), channel_id=1, source_target_pairs={{0,32},{16,48},{32,0},{48,16},{64,96},{80,112},{96,64},{112,80},{1... | collective-permute-start | bytes 786440 | tf_op jit(solution)/shard_map/ppermute | solution.py:16
  336.8 4.5 %collective-permute-done.3 = f32[128,512]{1,0:T(8,128)S(1)} collective-permute-done((f32[128,512]{1,0:T(8,128)S(1)}, f32[128,512]{1,0:T(8,128)S(1)}, u32[]{:S(2)}, u32[]{:S(2)}) %collective-permute-start.3) | collective-permute-done | bytes 262176 | tf_op jit(solution)/shard_map/ppermute | solution.py:16
  344.4 11.7 %cholesky.96 = f32[128,128]{1,0:T(8,128)S(1)} custom-call(f32[128,128]{1,0:T(8,128)S(1)} %fusion.84), custom_call_target="Cholesky" | custom-call | tf_op jit(solution)/shard_map/jit(cholesky)/cholesky | solution.py:40
  357.5 9.8 %custom-call.12 = f32[1,128,128]{1,2,0:T(8,128)S(1)} custom-call(f32[1,128,128]{2,1,0:T(8,128)S(1)} %fusion.73), custom_call_target="InvertDiagBlocksLowerTriangular" | custom-call | tf_op jit(solution)/shard_map/jit(_cho_solve)/triangular_solve | solution.py:41
  371.6 3.7 collective-permute-start.6
  375.3 4.9 %collective-permute-done.8 = f32[128,512]{1,0:T(8,128)S(1)} collective-permute-done((f32[128,512]{1,0:T(8,128)S(1)}, f32[128,512]{1,0:T(8,128)S(1)}, u32[]{:S(2)}, u32[]{:S(2)}) %collective-permute-start.8) | collective-permute-done | bytes 262176 | tf_op jit(solution)/shard_map/ppermute | solution.py:16
  380.3 3.6 collective-permute-done.6
  387.1 11.7 %cholesky.107 = f32[128,128]{1,0:T(8,128)S(1)} custom-call(f32[128,128]{1,0:T(8,128)S(1)} %fusion.79), custom_call_target="Cholesky" | custom-call | tf_op jit(solution)/shard_map/jit(cholesky)/cholesky | solution.py:40
  400.1 9.8 %custom-call.13 = f32[1,128,128]{1,2,0:T(8,128)S(1)} custom-call(f32[1,128,128]{2,1,0:T(8,128)S(1)} %fusion.74), custom_call_target="InvertDiagBlocksLowerTriangular" | custom-call | tf_op jit(solution)/shard_map/jit(_cho_solve)/triangular_solve | solution.py:41
  (117 shorter events, 60.4 us)
Async XLA Ops:
  7.2 194.8 %all-reduce.2.cloned.1.call-start = ((), (), s32[]{:S(2)}) async-start(), calls=%async_computation | async-start | bytes 524288 | tf_op jit(solution)/shard_map/psum | solution.py:68
  51.2 29.2 %copy-start.5 = (bf16[512,512]{1,0:T(8,128)(2,1)S(1)}, bf16[512,512]{1,0:T(8,128)(2,1)}, u32[]{:S(2)}) copy-start(bf16[512,512]{1,0:T(8,128)(2,1)} %param.18) | copy-start | bytes 1572868
  80.4 9.4 %copy-start.2 = (s32[512]{0:T(512)S(1)}, s32[512]{0:T(512)}, u32[]{:S(2)}) copy-start(s32[512]{0:T(512)} %param.15) | copy-start | bytes 6148
  80.4 9.4 %copy-start.4 = (s32[512]{0:T(512)S(1)}, s32[512]{0:T(512)}, u32[]{:S(2)}) copy-start(s32[512]{0:T(512)} %param.17) | copy-start | bytes 6148
  80.4 9.4 %copy-start.6 = (s32[20]{0:T(128)S(1)}, s32[20]{0:T(128)}, u32[]{:S(2)}) copy-start(s32[20]{0:T(128)} %constant.261.clone) | copy-start | bytes 244
  80.4 13.5 %copy-start.3 = (s32[512]{0:T(512)S(1)}, s32[512]{0:T(512)}, u32[]{:S(2)}) copy-start(s32[512]{0:T(512)} %param.16) | copy-start | bytes 6148
  87.2 146.0 %copy-start.1 = (f32[3,512]{1,0:T(4,128)S(1)}, f32[3,512]{1,0:T(4,128)}, u32[]{:S(2)}) copy-start(f32[3,512]{1,0:T(4,128)} %param.14) | copy-start | bytes 18436
  88.4 189.8 %all-gather.3.cloned.1.call-start = ((), (), s32[]{:S(2)}) async-start(), calls=%async_computation.1 | async-start | bytes 4456448 | tf_op jit(solution)/shard_map/all_gather | solution.py:73
  202.0 82.3 %copy-start = (f32[128,512]{1,0:T(8,128)S(1)}, f32[128,512]{1,0:T(8,128)}, u32[]{:S(2)}) copy-start(f32[128,512]{1,0:T(8,128)} %all-reduce.2.cloned.1.call-done) | copy-start | bytes 786436
  260.8 10.9 %collective-permute-start.1 = (f32[3,128]{1,0:T(4,128)S(1)}, f32[3,128]{1,0:T(4,128)S(1)}, u32[]{:S(2)}, u32[]{:S(2)}) collective-permute-start(f32[3,128]{1,0:T(4,128)S(1)} %psum.15), channel_id=1, source_target_pairs={{0,16},{16,0},{32,48},{48,32},{64,80},{80,64},{96,112},{112,96},{1... | collective-permute-start | bytes 4616 | tf_op jit(solution)/shard_map/ppermute | solution.py:16
  271.9 14.8 %collective-permute-start.4 = (f32[3,128]{1,0:T(4,128)S(1)}, f32[3,128]{1,0:T(4,128)S(1)}, u32[]{:S(2)}, u32[]{:S(2)}) collective-permute-start(f32[3,128]{1,0:T(4,128)S(1)} %fusion.66), channel_id=1, source_target_pairs={{0,32},{16,48},{32,0},{48,16},{64,96},{80,112},{96,64},{112,80},{1... | collective-permute-start | bytes 4616 | tf_op jit(solution)/shard_map/ppermute | solution.py:16
  280.8 11.1 %collective-permute-start.2 = (f32[128,512]{1,0:T(8,128)S(1)}, f32[128,512]{1,0:T(8,128)S(1)}, u32[]{:S(2)}, u32[]{:S(2)}) collective-permute-start(f32[128,512]{1,0:T(8,128)S(1)} %reduce_sum.30), channel_id=1, source_target_pairs={{0,16},{16,0},{32,48},{48,32},{64,80},{80,64},{96,112},{112,96},{1... | collective-permute-start | bytes 786440 | tf_op jit(solution)/shard_map/ppermute | solution.py:16
  284.2 12.5 %collective-permute-start = (f32[128,512]{1,0:T(8,128)S(1)}, f32[128,512]{1,0:T(8,128)S(1)}, u32[]{:S(2)}, u32[]{:S(2)}) collective-permute-start(f32[128,512]{1,0:T(8,128)S(1)} %copy-done), channel_id=1, source_target_pairs={{0,16},{16,0},{32,48},{48,32},{64,80},{80,64},{96,112},{112,96},{1... | collective-permute-start | bytes 786440 | tf_op jit(solution)/shard_map/ppermute | solution.py:16
  324.6 12.1 %collective-permute-start.5 = (f32[128,512]{1,0:T(8,128)S(1)}, f32[128,512]{1,0:T(8,128)S(1)}, u32[]{:S(2)}, u32[]{:S(2)}) collective-permute-start(f32[128,512]{1,0:T(8,128)S(1)} %fusion.25), channel_id=1, source_target_pairs={{0,32},{16,48},{32,0},{48,16},{64,96},{80,112},{96,64},{112,80},{1... | collective-permute-start | bytes 786440 | tf_op jit(solution)/shard_map/ppermute | solution.py:16
  329.5 11.8 %collective-permute-start.3 = (f32[128,512]{1,0:T(8,128)S(1)}, f32[128,512]{1,0:T(8,128)S(1)}, u32[]{:S(2)}, u32[]{:S(2)}) collective-permute-start(f32[128,512]{1,0:T(8,128)S(1)} %convolution_multiply_fusion.2), channel_id=1, source_target_pairs={{0,32},{16,48},{32,0},{48,16},{64,96},{80,112},{96,64},{112,80},{1... | collective-permute-start | bytes 786440 | tf_op jit(solution)/shard_map/ppermute | solution.py:16
  332.2 39.3 %collective-permute-start.7 = (f32[3,128]{1,0:T(4,128)S(1)}, f32[3,128]{1,0:T(4,128)S(1)}, u32[]{:S(2)}, u32[]{:S(2)}) collective-permute-start(f32[3,128]{1,0:T(4,128)S(1)} %fusion.67), channel_id=1, source_target_pairs={{0,64},{16,80},{32,96},{48,112},{64,0},{80,16},{96,32},{112,48},{1... | collective-permute-start | bytes 4616 | tf_op jit(solution)/shard_map/ppermute | solution.py:16
  369.1 11.1 %collective-permute-start.8 = (f32[128,512]{1,0:T(8,128)S(1)}, f32[128,512]{1,0:T(8,128)S(1)}, u32[]{:S(2)}, u32[]{:S(2)}) collective-permute-start(f32[128,512]{1,0:T(8,128)S(1)} %fusion.29), channel_id=1, source_target_pairs={{0,64},{16,80},{32,96},{48,112},{64,0},{80,16},{96,32},{112,48},{1... | collective-permute-start | bytes 786440 | tf_op jit(solution)/shard_map/ppermute | solution.py:16
  371.6 12.3 %collective-permute-start.6 = (f32[128,512]{1,0:T(8,128)S(1)}, f32[128,512]{1,0:T(8,128)S(1)}, u32[]{:S(2)}, u32[]{:S(2)}) collective-permute-start(f32[128,512]{1,0:T(8,128)S(1)} %convolution_multiply_fusion.1), channel_id=1, source_target_pairs={{0,64},{16,80},{32,96},{48,112},{64,0},{80,16},{96,32},{112,48},{1... | collective-permute-start | bytes 786440 | tf_op jit(solution)/shard_map/ppermute | solution.py:16
Sparse Core Ops, SparseCore 0:
  88.5 113.3 all-reduce.1
  233.3 44.8 all-gather.2
